TPU v7x, 32 devices: a whole 2x2x4 slice. The times are simulated.
32 devices in a mesh: view: 4 (over z), cell: 8 (over y, x, core).
Axes of the slice: x: 2, y: 2, z: 4, core: 2. Of those that a mesh axis runs over, the one named last changes fastest.
Arguments:
- params: float32 [59, 65536], P(None, 'cell'), may hold values from -6.22 to 3.2, as said below
- camera: float32 [4, 11], P('view'), may hold values from -0.3 to 1536, as said below
- targets: float32 [4, 256, 3, 256], P('view', 'cell'), may hold values from 0 to 1
- send_blocks: int32 [4, 8, 8, 16], P('view', 'cell'), may hold values from 0 to 255, as said below
- tile_blocks: int32 [4, 256, 16], P('view', 'cell'), may hold values from -1 to 127, as said below
- tile_order: int32 [4, 256, 512], P('view', 'cell'), may hold values from 0 to 511, as said below
Outputs:
- image: float32 [4, 256, 3, 256], P('view', 'cell')
- grads: float32 [59, 65536], P(None, 'cell')
Inputs may be any that keep to these rules, and one draw needn't show every extreme that they name: `params`: rows 0 to 2 lie in -3.2 to 3.2, rows 3 to 5 in log 0.002 to log 0.025, row 6 in 1 to 2, rows 7 to 9 in -1 to 1, row 10 in -3 to 2, rows 11 to 58 in -1.5 to 1.5. `camera`: quaternion first entry 1 to 2, its others -0.15 to 0.15, first two translation entries -0.3 to 0.3, third translation entry 4.5 to 6, focal lengths 2 to 3 times 16 max(32, 256 div 32), principal point within 20 of the image centre. `send_blocks`: the 16 numbers for one view, owner and receiving device are distinct. `tile_blocks`: A tile's live entries are distinct and come first, -1 fills the rest, and every tile has at least one live entry. `tile_order`: each tile's row is a permutation of 0 to 511.
All inputs are finite; a program needn't handle non-finite values.
Results may differ from a plain program's by a relative error of at most 0.0003.
Values sent between devices are 32-bit elements; how exact they have to be, the bound alone decides.
A program may use at most 128 MiB of HBM per device.

v0:
```python
import jax
import numpy as np
import jax.numpy as jnp
from jax import lax
from jax.experimental import pallas as pl
from jax.experimental.pallas import tpu as pltpu
from jax.sharding import PartitionSpec as P

BLOCK_GAUSSIANS = 32
TX = 32


HIGHEST_PRECISE = lax.Precision.HIGHEST
SH_ZERO = 0.28209479177387814
SH_ONE = 0.4886025119029199
SH_TWO = [
    1.0925484305920792,
    -1.0925484305920792,
    0.31539156525252005,
    -1.0925484305920792,
    0.5462742152960396,
]
SH_THREE = [
    -0.5900435899266435,
    2.890611442640554,
    -0.4570457994644658,
    0.3731763325901154,
    -0.4570457994644658,
    1.445305721320277,
    -0.5900435899266435,
]


def quat_matrix(qw, qx, qy, qz):
    return [
        [1.0 - 2.0 * (qy * qy + qz * qz), 2.0 * (qx * qy - qw * qz), 2.0 * (qx * qz + qw * qy)],
        [2.0 * (qx * qy + qw * qz), 1.0 - 2.0 * (qx * qx + qz * qz), 2.0 * (qy * qz - qw * qx)],
        [2.0 * (qx * qz - qw * qy), 2.0 * (qy * qz + qw * qx), 1.0 - 2.0 * (qx * qx + qy * qy)],
    ]


def sh_basis(dirx, diry, dirz):
    xx, yy, zz = (dirx * dirx, diry * diry, dirz * dirz)
    return [
        SH_ZERO + 0.0 * dirx,
        -SH_ONE * diry,
        SH_ONE * dirz,
        -SH_ONE * dirx,
        SH_TWO[0] * dirx * diry,
        SH_TWO[1] * diry * dirz,
        SH_TWO[2] * (2.0 * zz - xx - yy),
        SH_TWO[3] * dirx * dirz,
        SH_TWO[4] * (xx - yy),
        SH_THREE[0] * diry * (3.0 * xx - yy),
        SH_THREE[1] * dirx * diry * dirz,
        SH_THREE[2] * diry * (4.0 * zz - xx - yy),
        SH_THREE[3] * dirz * (2.0 * zz - 3.0 * xx - 3.0 * yy),
        SH_THREE[4] * dirx * (4.0 * zz - xx - yy),
        SH_THREE[5] * dirz * (xx - yy),
        SH_THREE[6] * dirx * (xx - 3.0 * yy),
    ]


def project(gauss, camera_row):
    cam_norm = jnp.sqrt(
        camera_row[0] * camera_row[0]
        + camera_row[1] * camera_row[1]
        + camera_row[2] * camera_row[2]
        + camera_row[3] * camera_row[3]
    )
    cam_quat = [camera_row[i] / cam_norm for i in range(4)]
    rotation = quat_matrix(cam_quat[0], cam_quat[1], cam_quat[2], cam_quat[3])
    focal_x, focal_y, centre_x, centre_y = (
        camera_row[7],
        camera_row[8],
        camera_row[9],
        camera_row[10],
    )
    cam_pos = [
        rotation[i][0] * gauss[0]
        + rotation[i][1] * gauss[1]
        + rotation[i][2] * gauss[2]
        + camera_row[4 + i]
        for i in range(3)
    ]
    inverse = 1.0 / cam_pos[2]
    screen_u = focal_x * cam_pos[0] * inverse + centre_x
    screen_w = focal_y * cam_pos[1] * inverse + centre_y
    gauss_norm = jnp.sqrt(
        gauss[6] * gauss[6] + gauss[7] * gauss[7] + gauss[8] * gauss[8] + gauss[9] * gauss[9]
    )
    grot = quat_matrix(
        gauss[6] / gauss_norm, gauss[7] / gauss_norm, gauss[8] / gauss_norm, gauss[9] / gauss_norm
    )
    scales = [jnp.exp(gauss[3 + k]) for k in range(3)]
    axes_cam = [
        [
            rotation[i][0] * grot[0][k] + rotation[i][1] * grot[1][k] + rotation[i][2] * grot[2][k]
            for k in range(3)
        ]
        for i in range(3)
    ]
    row_one = [
        (
            focal_x * inverse * axes_cam[0][k]
            - focal_x * cam_pos[0] * inverse * inverse * axes_cam[2][k]
        )
        * scales[k]
        for k in range(3)
    ]
    row_two = [
        (
            focal_y * inverse * axes_cam[1][k]
            - focal_y * cam_pos[1] * inverse * inverse * axes_cam[2][k]
        )
        * scales[k]
        for k in range(3)
    ]
    entry_a = row_one[0] * row_one[0] + row_one[1] * row_one[1] + row_one[2] * row_one[2] + 0.3
    entry_b = row_one[0] * row_two[0] + row_one[1] * row_two[1] + row_one[2] * row_two[2]
    entry_c = row_two[0] * row_two[0] + row_two[1] * row_two[1] + row_two[2] * row_two[2] + 0.3
    determinant = entry_a * entry_c - entry_b * entry_b
    opacity = -jnp.log(1.0 + jnp.exp(-gauss[10]))
    distance = jnp.sqrt(cam_pos[0] * cam_pos[0] + cam_pos[1] * cam_pos[1] + cam_pos[2] * cam_pos[2])
    direction = [
        (rotation[0][j] * cam_pos[0] + rotation[1][j] * cam_pos[1] + rotation[2][j] * cam_pos[2])
        / distance
        for j in range(3)
    ]
    basis = sh_basis(direction[0], direction[1], direction[2])
    colors = []
    for channel in range(3):
        accum = 0.5 + basis[0] * gauss[11 + channel]
        for order in range(1, 16):
            accum = accum + basis[order] * gauss[11 + 3 * order + channel]
        colors.append(jnp.maximum(accum, 0.0))
    return [
        screen_u,
        screen_w,
        entry_c / determinant,
        -entry_b / determinant,
        entry_a / determinant,
        opacity,
    ] + colors


TILE = 16
GROUP = 8
ROWS = 16
FIELDS = 9
NT_DIMS = (((1,), (1,)), ((), ()))


def pieces3(values):
    one = values.astype(jnp.bfloat16).astype(jnp.float32)
    rest = values - one
    two = rest.astype(jnp.bfloat16).astype(jnp.float32)
    return one, two, rest - two


def basis_rows(pixels):
    ids = np.arange(pixels)
    px = ids % TILE + 0.5 - TILE / 2
    py = ids // TILE + 0.5 - TILE / 2
    return np.stack([np.ones(pixels), px, py, px * px, px * py, py * py]).astype(np.float32)


def composite_kernel(
    slots_ref, first_ref, tab_ref, ord_ref, tgt_ref, wmat_ref, bas_ref, img_ref, gt_ref,
    p_s, f_s, x_s, m_s, w_s, y_s,
):
    group = pl.program_id(0)
    length = ord_ref.shape[1]
    pixels = tgt_ref.shape[2]
    entries = slots_ref.shape[1]
    per = 128 // BLOCK_GAUSSIANS

    @pl.when(group == 0)
    def _():
        gt_ref[...] = jnp.zeros_like(gt_ref)

    lane_part = lax.broadcasted_iota(jnp.int32, (ROWS, 128), 1) // BLOCK_GAUSSIANS
    lane_ids = lax.broadcasted_iota(jnp.int32, (length, length), 1)
    tile0 = first_ref[0] + group * GROUP

    def centre(t):
        tile = tile0 + t
        cx = (lax.rem(tile, TX) * TILE + TILE // 2).astype(jnp.float32)
        cy = (lax.div(tile, TX) * TILE + TILE // 2).astype(jnp.float32)
        return cx, cy

    for t in range(GROUP):
        cols = []
        for v in range(entries // per):
            chunk = None
            for b in range(per):
                block = tab_ref[slots_ref[group * GROUP + t, v * per + b]]
                chunk = block if chunk is None else jnp.where(lane_part == b, block, chunk)
            cols.append(chunk)
        fields = jnp.concatenate(cols, axis=1)
        cx, cy = centre(t)
        u = fields[0:1] - cx
        w = fields[1:2] - cy
        con_a, con_b, con_c, logo = fields[2:3], fields[3:4], fields[4:5], fields[5:6]
        f_s[t] = fields
        coefs = jnp.concatenate(
            [
                logo - 0.5 * (con_a * u * u + con_c * w * w) - con_b * u * w,
                con_a * u + con_b * w,
                con_c * w + con_b * u,
                -0.5 * con_a,
                -con_b,
                -0.5 * con_c,
                fields[6:9],
                jnp.zeros((ROWS - FIELDS, length), jnp.float32),
            ],
            axis=0,
        )
        parts = jnp.concatenate(
            list(pieces3(coefs)) + [jnp.zeros((128 - 3 * ROWS, length), jnp.float32)], axis=0
        ).astype(jnp.bfloat16)
        perm = jnp.where(ord_ref[0, :, t : t + 1] == lane_ids, 1.0, 0.0).astype(jnp.bfloat16)
        p_s[t] = perm
        x_s[pl.ds(t, length, stride=GROUP), :] = lax.dot_general(
            perm, parts, NT_DIMS, preferred_element_type=jnp.float32
        )

    rows = 64 * GROUP
    steps = length * GROUP // rows

    @pl.loop(0, steps)
    def _(c):
        part = pl.ds(pl.multiple_of(c * rows, rows), rows)
        m_s[part, :] = jnp.dot(
            x_s[part, :].astype(jnp.bfloat16), wmat_ref[...], preferred_element_type=jnp.float32
        )

    def twice(x):
        return jnp.concatenate([x] * (pixels // 128), axis=1)

    def load_colors(r):
        return [twice(m_s[r, pixels + 128 * ch : pixels + 128 * (ch + 1)]) for ch in range(3)]

    def forward(k, carry):
        trans, acc = carry
        r = pl.ds(pl.multiple_of(k * GROUP, GROUP), GROUP)
        alpha = jnp.exp(m_s[r, 0:pixels])
        weight = alpha * trans
        m_s[r, 0:pixels] = alpha
        w_s[r, :] = weight
        colors = load_colors(r)
        acc = tuple(a + c * weight for a, c in zip(acc, colors))
        return (trans - weight, acc)

    zero = jnp.zeros((GROUP, pixels), jnp.float32)
    _, image = lax.fori_loop(0, length, forward, (zero + 1.0, (zero, zero, zero)), unroll=8)
    glist = []
    for ch in range(3):
        img_ref[ch] = image[ch]
        glist.append((image[ch] - tgt_ref[ch]) * (1.0 / pixels))

    def backward(i, carry):
        k = length - 1 - i
        r = pl.ds(pl.multiple_of(k * GROUP, GROUP), GROUP)
        alpha = m_s[r, 0:pixels]
        weight = w_s[r, :]
        c = load_colors(r)
        dot = c[0] * glist[0] + c[1] * glist[1] + c[2] * glist[2]
        term = weight * dot
        m_s[r, 0:pixels] = term - carry * (alpha / (1.0 - alpha))
        return carry + term

    lax.fori_loop(0, length, backward, zero, unroll=8)

    grows = jnp.concatenate(
        [jnp.zeros((16, pixels), jnp.float32)]
        + glist
        + [jnp.zeros((128 - 16 - 3 * GROUP, pixels), jnp.float32)],
        axis=0,
    )
    ghigh = grows.astype(jnp.bfloat16)
    glow = (grows - ghigh.astype(jnp.float32)).astype(jnp.bfloat16)

    def nt(a, b):
        return lax.dot_general(a, b, NT_DIMS, preferred_element_type=jnp.float32)

    @pl.loop(0, steps)
    def _(c):
        part = pl.ds(pl.multiple_of(c * rows, rows), rows)
        h = m_s[part, 0:pixels]
        weight = w_s[part, :]
        h1 = h.astype(jnp.bfloat16)
        h2 = (h - h1.astype(jnp.float32)).astype(jnp.bfloat16)
        w1 = weight.astype(jnp.bfloat16)
        w2 = (weight - w1.astype(jnp.float32)).astype(jnp.bfloat16)
        bas = bas_ref[...]
        y_s[part, :] = nt(h1, bas) + nt(h2, bas) + nt(w1, ghigh) + nt(w1, glow) + nt(w2, ghigh)

    used = 16 + 3 * GROUP
    for t in range(GROUP):
        moments = y_s[pl.ds(t, length, stride=GROUP), :].T[0:used]
        stacked = jnp.concatenate(
            list(pieces3(moments)) + [jnp.zeros((128 - 3 * used, length), jnp.float32)], axis=0
        ).astype(jnp.bfloat16)
        back = jnp.dot(stacked, p_s[t], preferred_element_type=jnp.float32)
        back = back[0:used] + back[used : 2 * used] + back[2 * used : 3 * used]
        fields = f_s[t]
        cx, cy = centre(t)
        u = fields[0:1] - cx
        w = fields[1:2] - cy
        con_a, con_b, con_c = fields[2:3], fields[3:4], fields[4:5]
        h0, hx, hy, hxx, hxy, hyy = [back[j : j + 1] for j in range(6)]
        sx = hx - u * h0
        sy = hy - w * h0
        sxx = hxx - 2.0 * u * hx + u * u * h0
        syy = hyy - 2.0 * w * hy + w * w * h0
        sxy = hxy - u * hy - w * hx + u * w * h0
        out = jnp.concatenate(
            [
                con_a * sx + con_b * sy,
                con_c * sy + con_b * sx,
                -0.5 * sxx,
                -sxy,
                -0.5 * syy,
                h0,
            ]
            + [back[16 + ch * GROUP + t : 17 + ch * GROUP + t] for ch in range(3)]
            + [jnp.zeros((ROWS - FIELDS, length), jnp.float32)],
            axis=0,
        )
        for e in range(entries):
            slot = slots_ref[group * GROUP + t, e]
            v, b = divmod(e, per)
            gt_ref[slot] += jnp.where(lane_part == b, out[:, v * 128 : (v + 1) * 128], 0.0)


def composite(table, slots, order, goal, first_tile):
    tiles, length = order.shape
    pixels = goal.shape[-1]
    groups = tiles // GROUP
    table_rows = table.shape[0]
    order_cols = jnp.transpose(order.reshape(groups, GROUP, length), (0, 2, 1))
    basis = basis_rows(pixels)
    wmat = np.zeros((128, pixels + 3 * 128), np.float32)
    for piece in range(3):
        wmat[piece * ROWS : piece * ROWS + 6, :pixels] = basis
        for ch in range(3):
            wmat[piece * ROWS + 6 + ch, pixels + 128 * ch : pixels + 128 * (ch + 1)] = 1.0
    bas = np.zeros((128, pixels), np.float32)
    bas[:6] = basis
    full = lambda g, *_: (0, 0)
    whole = lambda g, *_: (0, 0, 0)
    image, gtab = pl.pallas_call(
        composite_kernel,
        out_shape=(
            jax.ShapeDtypeStruct((3, tiles, pixels), jnp.float32),
            jax.ShapeDtypeStruct((table_rows, ROWS, 128), jnp.float32),
        ),
        grid_spec=pltpu.PrefetchScalarGridSpec(
            num_scalar_prefetch=2,
            grid=(groups,),
            in_specs=[
                pl.BlockSpec((table_rows, ROWS, 128), whole),
                pl.BlockSpec((1, length, GROUP), lambda g, *_: (g, 0, 0)),
                pl.BlockSpec((3, GROUP, pixels), lambda g, *_: (0, g, 0)),
                pl.BlockSpec(wmat.shape, full),
                pl.BlockSpec(bas.shape, full),
            ],
            out_specs=(
                pl.BlockSpec((3, GROUP, pixels), lambda g, *_: (0, g, 0)),
                pl.BlockSpec((table_rows, ROWS, 128), whole),
            ),
            scratch_shapes=[
                pltpu.VMEM((GROUP, length, length), jnp.bfloat16),
                pltpu.VMEM((GROUP, ROWS, length), jnp.float32),
                pltpu.VMEM((length * GROUP, 128), jnp.float32),
                pltpu.VMEM((length * GROUP, pixels + 3 * 128), jnp.float32),
                pltpu.VMEM((length * GROUP, pixels), jnp.float32),
                pltpu.VMEM((length * GROUP, 128), jnp.float32),
            ],
        ),
        compiler_params=pltpu.CompilerParams(
            dimension_semantics=("arbitrary",), vmem_limit_bytes=60 * 1024 * 1024
        ),
    )(
        slots,
        first_tile,
        table,
        order_cols,
        jnp.transpose(goal, (1, 0, 2)),
        jnp.asarray(wmat, jnp.bfloat16),
        jnp.asarray(bas, jnp.bfloat16),
    )
    return jnp.transpose(image, (1, 0, 2)), gtab


SUB = 8


def project_kernel(params_ref, cam_ref, out_ref):
    @pl.loop(0, params_ref.shape[1] // SUB)
    def _(r):
        part = pl.ds(pl.multiple_of(r * SUB, SUB), SUB)
        gauss = [params_ref[i, part, :] for i in range(params_ref.shape[0])]
        camera = [cam_ref[i * SUB : (i + 1) * SUB, :] for i in range(cam_ref.shape[0] // SUB)]
        for f, value in enumerate(project(gauss, camera)):
            out_ref[f, part, :] = value


def pullback_kernel(params_ref, grads_ref, out_ref):
    views = grads_ref.shape[0]
    depth = params_ref.shape[1]
    cam_base = FIELDS * depth
    cam_n = (grads_ref.shape[1] - cam_base) // SUB

    @pl.loop(0, depth // SUB)
    def _(r):
        part = pl.ds(pl.multiple_of(r * SUB, SUB), SUB)
        gauss = [params_ref[i, part, :] for i in range(params_ref.shape[0])]

        def every_view(values):
            out = []
            for v in range(views):
                camera = [
                    grads_ref[v, cam_base + i * SUB : cam_base + (i + 1) * SUB, :]
                    for i in range(cam_n)
                ]
                out.append(project(values, camera))
            return out

        _, pullback = jax.vjp(every_view, gauss)
        cotangents = [
            [
                grads_ref[v, pl.ds(pl.multiple_of(f * depth + r * SUB, SUB), SUB), :]
                for f in range(FIELDS)
            ]
            for v in range(views)
        ]
        for i, value in enumerate(pullback(cotangents)[0]):
            out_ref[i, part, :] = value


def exchange_kernel(views, mine_ref, out_ref, local_sem, send_sem, recv_sem):
    me = lax.axis_index("view")
    barrier = pltpu.get_barrier_semaphore()
    peers = [lax.rem(me + step, views) for step in range(1, views)]
    for peer in peers:
        pl.semaphore_signal(
            barrier, inc=1, device_id={"view": peer}, device_id_type=pl.DeviceIdType.MESH
        )
    pl.semaphore_wait(barrier, views - 1)
    copies = []
    for step, peer in enumerate(peers):
        copies.append(
            pltpu.make_async_remote_copy(
                src_ref=mine_ref,
                dst_ref=out_ref.at[me],
                send_sem=send_sem.at[step],
                recv_sem=recv_sem.at[step],
                device_id={"view": peer},
                device_id_type=pl.DeviceIdType.MESH,
            )
        )
    for copy in copies:
        copy.start()
    own = pltpu.make_async_copy(mine_ref, out_ref.at[me], local_sem)
    own.start()
    own.wait()
    for copy in copies:
        copy.wait()


def exchange_views(mine):
    views = lax.axis_size("view")
    return pl.pallas_call(
        lambda *refs: exchange_kernel(views, *refs),
        out_shape=jax.ShapeDtypeStruct((views,) + mine.shape, jnp.float32),
        in_specs=[pl.BlockSpec(memory_space=pl.ANY)],
        out_specs=pl.BlockSpec(memory_space=pl.ANY),
        scratch_shapes=[
            pltpu.SemaphoreType.DMA,
            pltpu.SemaphoreType.DMA((views - 1,)),
            pltpu.SemaphoreType.DMA((views - 1,)),
        ],
        compiler_params=pltpu.CompilerParams(collective_id=0, has_side_effects=True),
        name="exchange_views",
    )(mine)


def local(params, camera, targets, send_blocks, tile_blocks, tile_order):
    cells = lax.axis_size("cell")
    cell_index = lax.axis_index("cell")
    values_n, owned = params.shape
    owned_blocks = owned // BLOCK_GAUSSIANS
    per_peer = send_blocks.shape[3]
    slots_n = cells * per_peer
    block_values = FIELDS * BLOCK_GAUSSIANS
    picks = send_blocks[0, 0].reshape(-1)
    depth = owned // 128
    spread = params.reshape(values_n, depth, 128)
    cam_rows = jnp.broadcast_to(
        camera[0][:, None, None], (camera.shape[1], SUB, 128)
    ).reshape(camera.shape[1] * SUB, 128)
    fields = pl.pallas_call(
        project_kernel,
        out_shape=jax.ShapeDtypeStruct((FIELDS, depth, 128), jnp.float32),
        name="project",
    )(spread, cam_rows)
    by_block = jnp.transpose(
        fields.reshape(FIELDS, owned_blocks, BLOCK_GAUSSIANS), (1, 0, 2)
    ).reshape(owned_blocks, block_values)
    chosen = jnp.take(by_block, picks, axis=0).reshape(cells, per_peer * block_values)
    received = lax.all_to_all(chosen, "cell", split_axis=0, concat_axis=0, tiled=True)
    received = received.reshape(slots_n, FIELDS, BLOCK_GAUSSIANS)
    dummy = np.zeros((1, FIELDS, BLOCK_GAUSSIANS), np.float32)
    dummy[:, 5] = -1e30
    table = jnp.concatenate([received, jnp.asarray(dummy)], axis=0)
    table = jnp.tile(
        jnp.pad(table, ((0, 0), (0, ROWS - FIELDS), (0, 0))), (1, 1, 128 // BLOCK_GAUSSIANS)
    )
    blocks = tile_blocks[0]
    slots = jnp.where(blocks < 0, slots_n, blocks)
    first_tile = (cell_index * blocks.shape[0]).astype(jnp.int32).reshape(1)
    picture, gtab = composite(table, slots, tile_order[0], targets[0], first_tile)
    slot_grad = (
        gtab[:slots_n, :FIELDS]
        .reshape(slots_n, FIELDS, 128 // BLOCK_GAUSSIANS, BLOCK_GAUSSIANS)
        .sum(2)
        .reshape(cells, per_peer * block_values)
    )
    returned = lax.all_to_all(slot_grad, "cell", split_axis=0, concat_axis=0, tiled=True)
    chosen_of = (jnp.arange(owned_blocks)[:, None] == picks[None, :]).astype(jnp.float32)
    summed = jnp.dot(
        chosen_of, returned.reshape(slots_n, block_values), precision=HIGHEST_PRECISE
    )
    summed = jnp.transpose(
        summed.reshape(owned_blocks, FIELDS, BLOCK_GAUSSIANS), (1, 0, 2)
    ).reshape(FIELDS * depth, 128)
    by_view = exchange_views(jnp.concatenate([summed, cam_rows], axis=0))
    total = pl.pallas_call(
        pullback_kernel,
        out_shape=jax.ShapeDtypeStruct((values_n, depth, 128), jnp.float32),
        name="pullback",
    )(spread, by_view)
    return (picture[None], total.reshape(values_n, owned))


def solution(mesh):
    return jax.shard_map(
        local,
        mesh=mesh,
        in_specs=(
            P(None, "cell"),
            P("view", None),
            P("view", "cell", None, None),
            P("view", "cell", None, None),
            P("view", "cell", None),
            P("view", "cell", None),
        ),
        out_specs=(P("view", "cell", None, None), P(None, "cell")),
        check_vma=False,
    )
```

profile of v0, /device:TPU:9, one launch (start us, length us, event | category | flops | bytes accessed | tf_op | source)
XLA Modules:
  0.0 174.9 jit_solution(2297420733734572329)
XLA Ops:
  0.6 0.7 compare_and_fusion
  1.3 0.8 reshape_squeeze.11
  2.1 0.1 broadcast_in_dim.32
  2.2 0.1 broadcast_in_dim.33
  2.3 2.0 %copy.35 = f32[8,8,64,128]{3,2,1,0:T(8,128)S(1)} copy(f32[8,8,64,128]{3,1,2,0:T(8,128)} %bitcast.46) | data formatting | bytes 4194304
  4.3 0.0 copy-start.5
  4.3 1.4 slice.6.params_ref
  5.7 0.1 broadcast_in_dim.35
  5.8 0.1 broadcast_in_dim.36
  5.9 0.7 broadcast_in_dim.37.cam_ref
  6.6 3.0 %project.1 = f32[9,64,128]{2,1,0:T(8,128)} custom-call(f32[59,64,128]{2,1,0:T(8,128)} %slice.6.params_ref, f32[88,128]{1,0:T(8,128)} %broadcast_in_dim.37.cam_ref), custom_call_target="tpu_custom_call" | custom-call | tf_op jit(solution)/shard_map/project/pallas_call | solution.py:504
  9.5 1.2 reshape.107
  10.8 0.3 copy.24
  11.1 0.0 copy-start.2
  11.1 0.2 copy.25
  11.3 0.8 gather_fusion
  12.1 0.1 gather.7
  12.3 0.8 copy.26
  13.1 4.4 %all-to-all-start = ((f32[8,1,4608]{2,1,0:T(1,128)}), f32[8,1,4608]{2,1,0:T(1,128)S(1)}, u32[]{:S(2)}, u32[]{:S(2)}) async-start(f32[8,1,4608]{2,1,0:T(1,128)} %copy.26), calls=%async_computation | async-start | bytes 294912 | tf_op jit(solution)/shard_map/all_to_all | solution.py:513
  17.5 0.1 copy.23
  17.5 1.3 copy.28
  18.9 0.6 compare_select_fusion.slots_ref
  19.5 2.7 %all-to-all-done = f32[8,1,4608]{2,1,0:T(1,128)S(1)} async-done(((f32[8,1,4608]{2,1,0:T(1,128)}), f32[8,1,4608]{2,1,0:T(1,128)S(1)}, u32[]{:S(2)}, u32[]{:S(2)}) %all-to-all-start) | async-done | bytes 147488 | tf_op jit(solution)/shard_map/all_to_all | solution.py:513
  22.2 0.3 reduce
  22.5 0.3 reshape.109
  22.8 0.3 copy.27
  23.2 0.2 tile.4
  23.4 1.7 copy.29.tab_ref
  25.1 89.8 %shard_map.104 = (f32[3,32,256]{2,1,0:T(8,128)}, f32[129,16,128]{2,1,0:T(8,128)}) custom-call(s32[32,16]{1,0:T(8,128)} %compare_select_fusion.slots_ref, s32[1]{0:T(128)} %bitcast.1.first_ref, f32[129,16,128]{2,1,0:T(8,128)} %copy.29.tab_ref, s32[4,512,8]{2,1,0:T(8,128)} %bitcast.44, f32[3,32,256]{2,1,0:T(8,128)} %bitcast.51, ...), custom_call_target="tpu_custom_call" | custom-call | tf_op jit(solution)/shard_map/pallas_call | solution.py:353
  114.9 1.3 slice.3
  116.2 0.3 copy.30
  116.5 0.0 copy-start.3
  116.6 0.5 copy.31
  117.0 1.0 all_to_all.13
  118.0 4.2 %all-to-all-start.1 = ((f32[8,1,4608]{2,1,0:T(1,128)}), f32[8,1,4608]{2,1,0:T(1,128)S(1)}, u32[]{:S(2)}, u32[]{:S(2)}) async-start(f32[8,1,4608]{2,1,0:T(1,128)} %all_to_all.13), calls=%async_computation.1 | async-start | bytes 294912 | tf_op jit(solution)/shard_map/all_to_all | solution.py:531
  122.2 0.1 reshape_squeeze.13
  122.3 4.7 %all-to-all-done.1 = f32[8,1,4608]{2,1,0:T(1,128)S(1)} async-done(((f32[8,1,4608]{2,1,0:T(1,128)}), f32[8,1,4608]{2,1,0:T(1,128)S(1)}, u32[]{:S(2)}, u32[]{:S(2)}) %all-to-all-start.1) | async-done | bytes 147488 | tf_op jit(solution)/shard_map/all_to_all | solution.py:531
  127.0 0.3 reduce.1
  127.3 0.1 reshape.111
  127.5 0.1 copy.33
  127.6 0.3 convolution_bitcast_fusion
  127.9 0.4 copy.34
  128.3 0.3 reshape.112
  128.6 0.7 pad_maximum_fusion.refs_0_
  129.3 33.2 %exchange_views.1.grads_ref = f32[4,664,128]{2,1,0:T(8,128)} custom-call(f32[664,128]{1,0:T(8,128)} %pad_maximum_fusion.refs_0_), custom_call_target="tpu_custom_call" | custom-call | tf_op jit(solution)/shard_map/exchange_views/pallas_call | solution.py:475
  162.6 8.1 %pullback.1 = f32[59,64,128]{2,1,0:T(8,128)} custom-call(f32[59,64,128]{2,1,0:T(8,128)} %slice.6.params_ref, f32[4,664,128]{2,1,0:T(8,128)} %exchange_views.1.grads_ref), custom_call_target="tpu_custom_call" | custom-call | tf_op jit(solution)/shard_map/pullback/pallas_call | solution.py:540
  170.7 1.7 pad.12
  172.4 2.5 %copy.36 = f32[8,8,64,128]{3,1,2,0:T(8,128)} copy(f32[8,8,64,128]{3,2,1,0:T(8,128)S(1)} %bitcast.41) | data formatting | bytes 4194304
  (14 shorter events, 0.1 us)
Async XLA Ops:
  4.3 1.4 copy-start.5
  11.1 6.3 %copy-start.4 = (s32[1,32,16]{1,2,0:T(8,128)S(1)}, s32[1,32,16]{1,2,0:T(8,128)}, u32[]{:S(2)}) copy-start(s32[1,32,16]{1,2,0:T(8,128)} %param.13) | copy-start | bytes 6148
  11.1 6.4 %copy-start.2 = (s32[1,32,512]{2,1,0:T(8,128)S(1)}, s32[1,32,512]{2,1,0:T(8,128)}, u32[]{:S(2)}) copy-start(s32[1,32,512]{2,1,0:T(8,128)} %param.14) | copy-start | bytes 196612
  13.1 9.1 %all-to-all-start = ((f32[8,1,4608]{2,1,0:T(1,128)}), f32[8,1,4608]{2,1,0:T(1,128)S(1)}, u32[]{:S(2)}, u32[]{:S(2)}) async-start(f32[8,1,4608]{2,1,0:T(1,128)} %copy.26), calls=%async_computation | async-start | bytes 294912 | tf_op jit(solution)/shard_map/all_to_all | solution.py:513
  17.5 5.7 %copy-start.1 = (f32[1,9,32]{0,2,1:T(8,128)S(1)}, f32[1,9,32]{0,2,1:T(8,128)}, u32[]{:S(2)}) copy-start(f32[1,9,32]{0,2,1:T(8,128)} %constant.35.clone) | copy-start | bytes 3460
  116.5 5.8 %copy-start.3 = (s32[1,1,8,16]{3,2,1,0:T(8,128)S(1)}, s32[1,1,8,16]{3,2,1,0:T(8,128)}, u32[]{:S(2)}) copy-start(s32[1,1,8,16]{3,2,1,0:T(8,128)} %param.12) | copy-start | bytes 1540
  118.0 9.0 %all-to-all-start.1 = ((f32[8,1,4608]{2,1,0:T(1,128)}), f32[8,1,4608]{2,1,0:T(1,128)S(1)}, u32[]{:S(2)}, u32[]{:S(2)}) async-start(f32[8,1,4608]{2,1,0:T(1,128)} %all_to_all.13), calls=%async_computation.1 | async-start | bytes 294912 | tf_op jit(solution)/shard_map/all_to_all | solution.py:531
  127.5 1.1 copy-start
where the time goes:
time: 176 us; the launch traced here: 175 us
  Pallas kernels  134 us (76%)
  local copies, waits for them, and re-layouts  20.9 us (12%)
  starting transfers between devices  8.61 us (5%)
  waiting for transfers between devices  7.36 us (4%)
  other arithmetic  2.84 us (2%)
    pallas_call x1, Pallas kernels, composite(): pl.pallas_call(composite_kernel, out_shape=(jax.ShapeDtypeStruct((3, tile...  89.8 us
    pallas_call x1, Pallas kernels, exchange_views(): pl.pallas_call(lambda *refs: exchange_kernel(views, *refs), out_shape=jax...  33.2 us
    pallas_call x1, Pallas kernels, local(): pl.pallas_call(pullback_kernel, out_shape=jax.ShapeDtypeStruct((values_n,...  8.12 us
    unnamed x16, local copies, waits for them, and re-layouts  6.32 us
    all_to_all x1, waiting for transfers between devices, local(): lax.all_to_all(slot_grad, 'cell', split_axis=0, concat_axis=0, tiled=True)  4.67 us
    all_to_all x1, starting transfers between devices, local(): lax.all_to_all(chosen, 'cell', split_axis=0, concat_axis=0, tiled=True)  4.39 us
    all_to_all x1, starting transfers between devices, local(): lax.all_to_all(slot_grad, 'cell', split_axis=0, concat_axis=0, tiled=True)  4.22 us
  transfers between devices with their start and end apart: 2, of which 2 were waited for; matrix products, arithmetic and copies ran while one was open for 1% of the time, Pallas kernels for 0%

commit v1 on v0

--- a/solution.py
+++ b/solution.py
@@ -402,7 +402,7 @@
     def _(r):
         part = pl.ds(pl.multiple_of(r * SUB, SUB), SUB)
         gauss = [params_ref[i, part, :] for i in range(params_ref.shape[0])]
-        camera = [cam_ref[i * SUB : (i + 1) * SUB, :] for i in range(cam_ref.shape[0] // SUB)]
+        camera = [cam_ref[i : i + 1, :] for i in range(cam_ref.shape[0])]
         for f, value in enumerate(project(gauss, camera)):
             out_ref[f, part, :] = value
 
@@ -411,7 +411,6 @@
     views = grads_ref.shape[0]
     depth = params_ref.shape[1]
     cam_base = FIELDS * depth
-    cam_n = (grads_ref.shape[1] - cam_base) // SUB
 
     @pl.loop(0, depth // SUB)
     def _(r):
@@ -421,10 +420,7 @@
         def every_view(values):
             out = []
             for v in range(views):
-                camera = [
-                    grads_ref[v, cam_base + i * SUB : cam_base + (i + 1) * SUB, :]
-                    for i in range(cam_n)
-                ]
+                camera = [grads_ref[v, i : i + 1, :] for i in range(cam_base, grads_ref.shape[1])]
                 out.append(project(values, camera))
             return out
 
@@ -443,26 +439,54 @@
 def exchange_kernel(views, mine_ref, out_ref, local_sem, send_sem, recv_sem):
     me = lax.axis_index("view")
     barrier = pltpu.get_barrier_semaphore()
+    right, left = lax.rem(me + 1, views), lax.rem(me + views - 1, views)
+    half = mine_ref.shape[0] // 2
+    parts = [pl.ds(0, half), pl.ds(half, mine_ref.shape[0] - half)]
+
+    def signal(peer):
+        pl.semaphore_signal(
+            barrier, inc=1, device_id={"view": peer}, device_id_type=pl.DeviceIdType.MESH
+        )
+
+    def send(src, owner, part, peer, index):
+        copy = pltpu.make_async_remote_copy(
+            src_ref=src.at[parts[part]],
+            dst_ref=out_ref.at[owner, parts[part]],
+            send_sem=send_sem.at[index],
+            recv_sem=recv_sem.at[index],
+            device_id={"view": peer},
+            device_id_type=pl.DeviceIdType.MESH,
+        )
+        copy.start()
+        return copy
+
+    if views == 4:
+        signal(right)
+        signal(left)
+        pl.semaphore_wait(barrier, 2)
+        first = send(mine_ref, me, 0, right, 0)
+        second = send(mine_ref, me, 1, left, 1)
+        copies = [first, second, send(mine_ref, me, 1, right, 2), send(mine_ref, me, 0, left, 3)]
+        own = pltpu.make_async_copy(mine_ref, out_ref.at[me], local_sem)
+        own.start()
+        first.wait_recv()
+        copies.append(send(out_ref.at[left], left, 0, right, 4))
+        second.wait_recv()
+        copies.append(send(out_ref.at[right], right, 1, left, 5))
+        first.wait_send()
+        second.wait_send()
+        for copy in copies[2:]:
+            copy.wait()
+        own.wait()
+        return
     peers = [lax.rem(me + step, views) for step in range(1, views)]
     for peer in peers:
-        pl.semaphore_signal(
-            barrier, inc=1, device_id={"view": peer}, device_id_type=pl.DeviceIdType.MESH
-        )
+        signal(peer)
     pl.semaphore_wait(barrier, views - 1)
     copies = []
     for step, peer in enumerate(peers):
-        copies.append(
-            pltpu.make_async_remote_copy(
-                src_ref=mine_ref,
-                dst_ref=out_ref.at[me],
-                send_sem=send_sem.at[step],
-                recv_sem=recv_sem.at[step],
-                device_id={"view": peer},
-                device_id_type=pl.DeviceIdType.MESH,
-            )
-        )
-    for copy in copies:
-        copy.start()
+        copies.append(send(mine_ref, me, 0, peer, 2 * step))
+        copies.append(send(mine_ref, me, 1, peer, 2 * step + 1))
     own = pltpu.make_async_copy(mine_ref, out_ref.at[me], local_sem)
     own.start()
     own.wait()
@@ -479,8 +503,8 @@
         out_specs=pl.BlockSpec(memory_space=pl.ANY),
         scratch_shapes=[
             pltpu.SemaphoreType.DMA,
-            pltpu.SemaphoreType.DMA((views - 1,)),
-            pltpu.SemaphoreType.DMA((views - 1,)),
+            pltpu.SemaphoreType.DMA((2 * views - 2,)),
+            pltpu.SemaphoreType.DMA((2 * views - 2,)),
         ],
         compiler_params=pltpu.CompilerParams(collective_id=0, has_side_effects=True),
         name="exchange_views",
@@ -499,8 +523,9 @@
     depth = owned // 128
     spread = params.reshape(values_n, depth, 128)
     cam_rows = jnp.broadcast_to(
-        camera[0][:, None, None], (camera.shape[1], SUB, 128)
-    ).reshape(camera.shape[1] * SUB, 128)
+        jnp.pad(camera[0], (0, -camera.shape[1] % SUB))[:, None],
+        (camera.shape[1] + -camera.shape[1] % SUB, 128),
+    )
     fields = pl.pallas_call(
         project_kernel,
         out_shape=jax.ShapeDtypeStruct((FIELDS, depth, 128), jnp.float32),

time: 176 us -> 167 us (0.949)
  Pallas kernels: 134 us -> 124 us
    pallas_call x1, Pallas kernels: 33.2 us -> 23.5 us  [exchange_views(): pl.pallas_call(lambda *refs: exchange_kernel(views, *refs), out_shape=jax...]
where the time goes in v1:
time: 167 us; the launch traced here: 165 us
  Pallas kernels  124 us (74%)
  local copies, waits for them, and re-layouts  20.8 us (12%)
  starting transfers between devices  8.6 us (5%)
  waiting for transfers between devices  7.36 us (4%)
  other arithmetic  2.84 us (2%)
    pallas_call x1, Pallas kernels, composite(): pl.pallas_call(composite_kernel, out_shape=(jax.ShapeDtypeStruct((3, tile...  89.8 us
    pallas_call x1, Pallas kernels, exchange_views(): pl.pallas_call(lambda *refs: exchange_kernel(views, *refs), out_shape=jax...  23.5 us
    pallas_call x1, Pallas kernels, local(): pl.pallas_call(pullback_kernel, out_shape=jax.ShapeDtypeStruct((values_n,...  8.04 us
    unnamed x16, local copies, waits for them, and re-layouts  6.32 us
    all_to_all x1, waiting for transfers between devices, local(): lax.all_to_all(slot_grad, 'cell', split_axis=0, concat_axis=0, tiled=True)  4.67 us
    all_to_all x1, starting transfers between devices, local(): lax.all_to_all(chosen, 'cell', split_axis=0, concat_axis=0, tiled=True)  4.39 us
    all_to_all x1, starting transfers between devices, local(): lax.all_to_all(slot_grad, 'cell', split_axis=0, concat_axis=0, tiled=True)  4.21 us
  transfers between devices with their start and end apart: 2, of which 2 were waited for; matrix products, arithmetic and copies ran while one was open for 1% of the time, Pallas kernels for 0%

profile of v1, /device:TPU:9, one launch (start us, length us, event | category | flops | bytes accessed | tf_op | source)
XLA Modules:
  0.0 165.0 jit_solution(14823143212132720817)
XLA Ops:
  0.6 0.8 reshape_squeeze.11
  1.4 0.7 compare_and_fusion
  2.1 2.0 %copy.35 = f32[8,8,64,128]{3,2,1,0:T(8,128)S(1)} copy(f32[8,8,64,128]{3,1,2,0:T(8,128)} %bitcast.46) | data formatting | bytes 4194304
  4.1 0.0 copy-start.5
  4.1 1.4 slice.6.params_ref
  5.5 0.0 copy-done.5
  5.5 0.7 broadcast_in_dim.29.cam_ref
  6.1 3.0 %project.1 = f32[9,64,128]{2,1,0:T(8,128)} custom-call(f32[59,64,128]{2,1,0:T(8,128)} %slice.6.params_ref, f32[16,128]{1,0:T(8,128)} %broadcast_in_dim.29.cam_ref), custom_call_target="tpu_custom_call" | custom-call | tf_op jit(solution)/shard_map/project/pallas_call | solution.py:529
  9.1 1.2 reshape.105
  10.4 0.3 copy.24
  10.7 0.2 copy.25
  10.9 0.0 copy-start.4
  10.9 0.8 gather_fusion
  11.7 0.1 gather.7
  11.8 0.1 broadcast_in_dim.27
  11.9 0.1 broadcast_in_dim.28
  12.1 0.8 copy.26
  12.9 4.4 %all-to-all-start = ((f32[8,1,4608]{2,1,0:T(1,128)}), f32[8,1,4608]{2,1,0:T(1,128)S(1)}, u32[]{:S(2)}, u32[]{:S(2)}) async-start(f32[8,1,4608]{2,1,0:T(1,128)} %copy.26), calls=%async_computation | async-start | bytes 294912 | tf_op jit(solution)/shard_map/all_to_all | solution.py:538
  17.3 1.3 copy.28
  18.6 0.1 copy.23
  18.7 0.6 compare_select_fusion.slots_ref
  19.3 2.7 %all-to-all-done = f32[8,1,4608]{2,1,0:T(1,128)S(1)} async-done(((f32[8,1,4608]{2,1,0:T(1,128)}), f32[8,1,4608]{2,1,0:T(1,128)S(1)}, u32[]{:S(2)}, u32[]{:S(2)}) %all-to-all-start) | async-done | bytes 147488 | tf_op jit(solution)/shard_map/all_to_all | solution.py:538
  22.0 0.3 reduce
  22.3 0.3 reshape.107
  22.7 0.3 copy.27
  23.0 0.2 tile.4
  23.3 1.7 %copy.29.tab_ref = f32[129,16,128]{2,1,0:T(8,128)} copy(f32[129,16,128]{0,2,1:T(8,128)S(1)} %bitcast.40) | data formatting | bytes 2113536 | tf_op jit(solution)/shard_map/tile | solution.py:543
  25.0 89.8 %shard_map.104 = (f32[3,32,256]{2,1,0:T(8,128)}, f32[129,16,128]{2,1,0:T(8,128)}) custom-call(s32[32,16]{1,0:T(8,128)} %compare_select_fusion.slots_ref, s32[1]{0:T(128)} %bitcast.1.first_ref, f32[129,16,128]{2,1,0:T(8,128)} %copy.29.tab_ref, s32[4,512,8]{2,1,0:T(8,128)} %bitcast.44, f32[3,32,256]{2,1,0:T(8,128)} %bitcast.51, ...), custom_call_target="tpu_custom_call" | custom-call | tf_op jit(solution)/shard_map/pallas_call | solution.py:353
  114.7 1.3 slice.3
  116.0 0.3 copy.30
  116.3 0.0 copy-start.3
  116.4 0.5 copy.31
  116.9 1.0 all_to_all.13
  117.9 4.2 %all-to-all-start.1 = ((f32[8,1,4608]{2,1,0:T(1,128)}), f32[8,1,4608]{2,1,0:T(1,128)S(1)}, u32[]{:S(2)}, u32[]{:S(2)}) async-start(f32[8,1,4608]{2,1,0:T(1,128)} %all_to_all.13), calls=%async_computation.1 | async-start | bytes 294912 | tf_op jit(solution)/shard_map/all_to_all | solution.py:556
  122.1 0.1 reshape_squeeze.13
  122.2 4.7 %all-to-all-done.1 = f32[8,1,4608]{2,1,0:T(1,128)S(1)} async-done(((f32[8,1,4608]{2,1,0:T(1,128)}), f32[8,1,4608]{2,1,0:T(1,128)S(1)}, u32[]{:S(2)}, u32[]{:S(2)}) %all-to-all-start.1) | async-done | bytes 147488 | tf_op jit(solution)/shard_map/all_to_all | solution.py:556
  126.8 0.3 reduce.1
  127.2 0.1 reshape.109
  127.3 0.1 copy.33
  127.4 0.3 convolution_bitcast_fusion
  127.7 0.4 copy.34
  128.1 0.3 reshape.110
  128.4 0.0 copy-done.1
  128.4 0.7 pad_maximum_fusion.refs_0_
  129.2 23.5 %exchange_views.1.grads_ref = f32[4,592,128]{2,1,0:T(8,128)} custom-call(f32[592,128]{1,0:T(8,128)} %pad_maximum_fusion.refs_0_), custom_call_target="tpu_custom_call" | custom-call | tf_op jit(solution)/shard_map/exchange_views/pallas_call | solution.py:499
  152.7 8.0 %pullback.1 = f32[59,64,128]{2,1,0:T(8,128)} custom-call(f32[59,64,128]{2,1,0:T(8,128)} %slice.6.params_ref, f32[4,592,128]{2,1,0:T(8,128)} %exchange_views.1.grads_ref), custom_call_target="tpu_custom_call" | custom-call | tf_op jit(solution)/shard_map/pullback/pallas_call | solution.py:565
  160.7 1.7 %pad.17 = f32[64,64,128]{2,1,0:T(8,128)S(1)} pad(f32[59,64,128]{2,1,0:T(8,128)} %pullback.1, f32[]{:T(128)} %constant.33.clone.1), padding=0_5x0_0x0_0 | pad | bytes 4030468
  162.5 2.5 %copy.36 = f32[8,8,64,128]{3,1,2,0:T(8,128)} copy(f32[8,8,64,128]{3,2,1,0:T(8,128)S(1)} %bitcast.41) | data formatting | bytes 4194304
  (13 shorter events, 0.1 us)
Async XLA Ops:
  4.1 1.4 copy-start.5
  10.7 6.6 %copy-start.2 = (s32[1,32,512]{2,1,0:T(8,128)S(1)}, s32[1,32,512]{2,1,0:T(8,128)}, u32[]{:S(2)}) copy-start(s32[1,32,512]{2,1,0:T(8,128)} %param.14) | copy-start | bytes 196612
  10.9 7.7 %copy-start.4 = (s32[1,32,16]{1,2,0:T(8,128)S(1)}, s32[1,32,16]{1,2,0:T(8,128)}, u32[]{:S(2)}) copy-start(s32[1,32,16]{1,2,0:T(8,128)} %param.13) | copy-start | bytes 6148
  12.9 9.1 %all-to-all-start = ((f32[8,1,4608]{2,1,0:T(1,128)}), f32[8,1,4608]{2,1,0:T(1,128)S(1)}, u32[]{:S(2)}, u32[]{:S(2)}) async-start(f32[8,1,4608]{2,1,0:T(1,128)} %copy.26), calls=%async_computation | async-start | bytes 294912 | tf_op jit(solution)/shard_map/all_to_all | solution.py:538
  17.3 5.7 %copy-start = (f32[1,9,32]{0,2,1:T(8,128)S(1)}, f32[1,9,32]{0,2,1:T(8,128)}, u32[]{:S(2)}) copy-start(f32[1,9,32]{0,2,1:T(8,128)} %constant.35.clone) | copy-start | bytes 3460
  116.3 5.7 %copy-start.3 = (s32[1,1,8,16]{3,2,1,0:T(8,128)S(1)}, s32[1,1,8,16]{3,2,1,0:T(8,128)}, u32[]{:S(2)}) copy-start(s32[1,1,8,16]{3,2,1,0:T(8,128)} %param.12) | copy-start | bytes 1540
  117.9 9.0 %all-to-all-start.1 = ((f32[8,1,4608]{2,1,0:T(1,128)}), f32[8,1,4608]{2,1,0:T(1,128)S(1)}, u32[]{:S(2)}, u32[]{:S(2)}) async-start(f32[8,1,4608]{2,1,0:T(1,128)} %all_to_all.13), calls=%async_computation.1 | async-start | bytes 294912 | tf_op jit(solution)/shard_map/all_to_all | solution.py:556
  127.3 1.1 copy-start.1

commit v2 on v1

--- a/solution.py
+++ b/solution.py
@@ -253,24 +253,22 @@
         return (trans - weight, acc)
 
     zero = jnp.zeros((GROUP, pixels), jnp.float32)
-    _, image = lax.fori_loop(0, length, forward, (zero + 1.0, (zero, zero, zero)), unroll=8)
+    _, image = lax.fori_loop(0, length, forward, (zero + 1.0, (zero, zero, zero)), unroll=16)
     glist = []
     for ch in range(3):
         img_ref[ch] = image[ch]
         glist.append((image[ch] - tgt_ref[ch]) * (1.0 / pixels))
 
-    def backward(i, carry):
+    def backward(i, behind):
         k = length - 1 - i
         r = pl.ds(pl.multiple_of(k * GROUP, GROUP), GROUP)
+        c = load_colors(r)
+        delta = (c[0] * glist[0] + c[1] * glist[1] + c[2] * glist[2]) - behind
         alpha = m_s[r, 0:pixels]
-        weight = w_s[r, :]
-        c = load_colors(r)
-        dot = c[0] * glist[0] + c[1] * glist[1] + c[2] * glist[2]
-        term = weight * dot
-        m_s[r, 0:pixels] = term - carry * (alpha / (1.0 - alpha))
-        return carry + term
-
-    lax.fori_loop(0, length, backward, zero, unroll=8)
+        m_s[r, 0:pixels] = w_s[r, :] * delta
+        return behind + alpha * delta
+
+    lax.fori_loop(0, length, backward, zero, unroll=16)
 
     grows = jnp.concatenate(
         [jnp.zeros((16, pixels), jnp.float32)]
@@ -280,6 +278,7 @@
     )
     ghigh = grows.astype(jnp.bfloat16)
     glow = (grows - ghigh.astype(jnp.float32)).astype(jnp.bfloat16)
+    gboth = jnp.concatenate([ghigh, glow], axis=0)
 
     def nt(a, b):
         return lax.dot_general(a, b, NT_DIMS, preferred_element_type=jnp.float32)
@@ -294,7 +293,10 @@
         w1 = weight.astype(jnp.bfloat16)
         w2 = (weight - w1.astype(jnp.float32)).astype(jnp.bfloat16)
         bas = bas_ref[...]
-        y_s[part, :] = nt(h1, bas) + nt(h2, bas) + nt(w1, ghigh) + nt(w1, glow) + nt(w2, ghigh)
+        both = nt(w1, gboth)
+        y_s[part, :] = (
+            nt(h1, bas) + nt(h2, bas) + nt(w2, ghigh) + both[:, 0:128] + both[:, 128:256]
+        )
 
     used = 16 + 3 * GROUP
     for t in range(GROUP):

time: 167 us -> 156 us (0.934)
  Pallas kernels: 124 us -> 113 us
    pallas_call x1, Pallas kernels: 89.8 us -> 78.2 us  [composite(): pl.pallas_call(composite_kernel, out_shape=(jax.ShapeDtypeStruct((3, tile...]
where the time goes in v2:
time: 156 us; the launch traced here: 153 us
  Pallas kernels  113 us (72%)
  local copies, waits for them, and re-layouts  20.8 us (13%)
  starting transfers between devices  8.63 us (6%)
  waiting for transfers between devices  7.36 us (5%)
  other arithmetic  2.84 us (2%)
    pallas_call x1, Pallas kernels, composite(): pl.pallas_call(composite_kernel, out_shape=(jax.ShapeDtypeStruct((3, tile...  78.2 us
    pallas_call x1, Pallas kernels, exchange_views(): pl.pallas_call(lambda *refs: exchange_kernel(views, *refs), out_shape=jax...  23.6 us
    pallas_call x1, Pallas kernels, local(): pl.pallas_call(pullback_kernel, out_shape=jax.ShapeDtypeStruct((values_n,...  8.04 us
    unnamed x16, local copies, waits for them, and re-layouts  6.32 us
    all_to_all x1, waiting for transfers between devices, local(): lax.all_to_all(slot_grad, 'cell', split_axis=0, concat_axis=0, tiled=True)  4.67 us
    all_to_all x1, starting transfers between devices, local(): lax.all_to_all(chosen, 'cell', split_axis=0, concat_axis=0, tiled=True)  4.39 us
    all_to_all x1, starting transfers between devices, local(): lax.all_to_all(slot_grad, 'cell', split_axis=0, concat_axis=0, tiled=True)  4.23 us
  transfers between devices with their start and end apart: 2, of which 2 were waited for; matrix products, arithmetic and copies ran while one was open for 1% of the time, Pallas kernels for 0%

profile of v2, /device:TPU:9, one launch (start us, length us, event | category | flops | bytes accessed | tf_op | source)
XLA Modules:
  0.0 153.5 jit_solution(14948127151860710466)
XLA Ops:
  0.6 0.8 reshape_squeeze.11
  1.4 0.7 compare_and_fusion
  2.1 2.0 %copy.35 = f32[8,8,64,128]{3,2,1,0:T(8,128)S(1)} copy(f32[8,8,64,128]{3,1,2,0:T(8,128)} %bitcast.46) | data formatting | bytes 4194304
  4.1 0.0 copy-start.5
  4.1 1.4 slice.6.params_ref
  5.5 0.0 copy-done.5
  5.5 0.7 broadcast_in_dim.29.cam_ref
  6.1 3.0 %project.1 = f32[9,64,128]{2,1,0:T(8,128)} custom-call(f32[59,64,128]{2,1,0:T(8,128)} %slice.6.params_ref, f32[16,128]{1,0:T(8,128)} %broadcast_in_dim.29.cam_ref), custom_call_target="tpu_custom_call" | custom-call | tf_op jit(solution)/shard_map/project/pallas_call | solution.py:531
  9.1 1.2 reshape.105
  10.4 0.3 copy.24
  10.7 0.2 copy.25
  10.9 0.0 copy-start.4
  10.9 0.8 gather_fusion
  11.7 0.1 gather.7
  11.8 0.1 broadcast_in_dim.27
  11.9 0.1 broadcast_in_dim.28
  12.1 0.8 copy.26
  12.9 4.4 %all-to-all-start = ((f32[8,1,4608]{2,1,0:T(1,128)}), f32[8,1,4608]{2,1,0:T(1,128)S(1)}, u32[]{:S(2)}, u32[]{:S(2)}) async-start(f32[8,1,4608]{2,1,0:T(1,128)} %copy.26), calls=%async_computation | async-start | bytes 294912 | tf_op jit(solution)/shard_map/all_to_all | solution.py:540
  17.3 1.3 copy.28
  18.6 0.0 copy-done.4
  18.6 0.1 copy.23
  18.7 0.6 compare_select_fusion.slots_ref
  19.3 2.7 %all-to-all-done = f32[8,1,4608]{2,1,0:T(1,128)S(1)} async-done(((f32[8,1,4608]{2,1,0:T(1,128)}), f32[8,1,4608]{2,1,0:T(1,128)S(1)}, u32[]{:S(2)}, u32[]{:S(2)}) %all-to-all-start) | async-done | bytes 147488 | tf_op jit(solution)/shard_map/all_to_all | solution.py:540
  22.0 0.3 reduce
  22.3 0.3 reshape.107
  22.7 0.3 copy.27
  23.0 0.2 tile.4
  23.3 1.7 %copy.29.tab_ref = f32[129,16,128]{2,1,0:T(8,128)} copy(f32[129,16,128]{0,2,1:T(8,128)S(1)} %bitcast.40) | data formatting | bytes 2113536 | tf_op jit(solution)/shard_map/tile | solution.py:545
  25.0 78.2 %shard_map.104 = (f32[3,32,256]{2,1,0:T(8,128)}, f32[129,16,128]{2,1,0:T(8,128)}) custom-call(s32[32,16]{1,0:T(8,128)} %compare_select_fusion.slots_ref, s32[1]{0:T(128)} %bitcast.1.first_ref, f32[129,16,128]{2,1,0:T(8,128)} %copy.29.tab_ref, s32[4,512,8]{2,1,0:T(8,128)} %bitcast.44, f32[3,32,256]{2,1,0:T(8,128)} %bitcast.51, ...), custom_call_target="tpu_custom_call" | custom-call | tf_op jit(solution)/shard_map/pallas_call | solution.py:355
  103.2 1.3 slice.3
  104.4 0.3 copy.30
  104.8 0.0 copy-start.3
  104.8 0.5 copy.31
  105.3 1.0 all_to_all.13
  106.3 4.2 %all-to-all-start.1 = ((f32[8,1,4608]{2,1,0:T(1,128)}), f32[8,1,4608]{2,1,0:T(1,128)S(1)}, u32[]{:S(2)}, u32[]{:S(2)}) async-start(f32[8,1,4608]{2,1,0:T(1,128)} %all_to_all.13), calls=%async_computation.1 | async-start | bytes 294912 | tf_op jit(solution)/shard_map/all_to_all | solution.py:558
  110.5 0.1 reshape_squeeze.13
  110.6 4.7 %all-to-all-done.1 = f32[8,1,4608]{2,1,0:T(1,128)S(1)} async-done(((f32[8,1,4608]{2,1,0:T(1,128)}), f32[8,1,4608]{2,1,0:T(1,128)S(1)}, u32[]{:S(2)}, u32[]{:S(2)}) %all-to-all-start.1) | async-done | bytes 147488 | tf_op jit(solution)/shard_map/all_to_all | solution.py:558
  115.3 0.3 reduce.1
  115.6 0.1 reshape.109
  115.8 0.1 copy.33
  115.9 0.3 convolution_bitcast_fusion
  116.2 0.4 copy.34
  116.6 0.3 reshape.110
  116.9 0.7 pad_maximum_fusion.refs_0_
  117.6 23.6 %exchange_views.1.grads_ref = f32[4,592,128]{2,1,0:T(8,128)} custom-call(f32[592,128]{1,0:T(8,128)} %pad_maximum_fusion.refs_0_), custom_call_target="tpu_custom_call" | custom-call | tf_op jit(solution)/shard_map/exchange_views/pallas_call | solution.py:501
  141.2 8.0 %pullback.1 = f32[59,64,128]{2,1,0:T(8,128)} custom-call(f32[59,64,128]{2,1,0:T(8,128)} %slice.6.params_ref, f32[4,592,128]{2,1,0:T(8,128)} %exchange_views.1.grads_ref), custom_call_target="tpu_custom_call" | custom-call | tf_op jit(solution)/shard_map/pullback/pallas_call | solution.py:567
  149.2 1.7 %pad.17 = f32[64,64,128]{2,1,0:T(8,128)S(1)} pad(f32[59,64,128]{2,1,0:T(8,128)} %pullback.1, f32[]{:T(128)} %constant.33.clone.1), padding=0_5x0_0x0_0 | pad | bytes 4030468
  151.0 2.5 %copy.36 = f32[8,8,64,128]{3,1,2,0:T(8,128)} copy(f32[8,8,64,128]{3,2,1,0:T(8,128)S(1)} %bitcast.41) | data formatting | bytes 4194304
  (13 shorter events, 0.1 us)
Async XLA Ops:
  4.1 1.4 copy-start.5
  10.7 6.6 %copy-start.2 = (s32[1,32,512]{2,1,0:T(8,128)S(1)}, s32[1,32,512]{2,1,0:T(8,128)}, u32[]{:S(2)}) copy-start(s32[1,32,512]{2,1,0:T(8,128)} %param.14) | copy-start | bytes 196612
  10.9 7.7 %copy-start.4 = (s32[1,32,16]{1,2,0:T(8,128)S(1)}, s32[1,32,16]{1,2,0:T(8,128)}, u32[]{:S(2)}) copy-start(s32[1,32,16]{1,2,0:T(8,128)} %param.13) | copy-start | bytes 6148
  12.9 9.1 %all-to-all-start = ((f32[8,1,4608]{2,1,0:T(1,128)}), f32[8,1,4608]{2,1,0:T(1,128)S(1)}, u32[]{:S(2)}, u32[]{:S(2)}) async-start(f32[8,1,4608]{2,1,0:T(1,128)} %copy.26), calls=%async_computation | async-start | bytes 294912 | tf_op jit(solution)/shard_map/all_to_all | solution.py:540
  17.3 5.7 %copy-start = (f32[1,9,32]{0,2,1:T(8,128)S(1)}, f32[1,9,32]{0,2,1:T(8,128)}, u32[]{:S(2)}) copy-start(f32[1,9,32]{0,2,1:T(8,128)} %constant.35.clone) | copy-start | bytes 3460
  104.8 5.8 %copy-start.3 = (s32[1,1,8,16]{3,2,1,0:T(8,128)S(1)}, s32[1,1,8,16]{3,2,1,0:T(8,128)}, u32[]{:S(2)}) copy-start(s32[1,1,8,16]{3,2,1,0:T(8,128)} %param.12) | copy-start | bytes 1540
  106.3 9.0 %all-to-all-start.1 = ((f32[8,1,4608]{2,1,0:T(1,128)}), f32[8,1,4608]{2,1,0:T(1,128)S(1)}, u32[]{:S(2)}, u32[]{:S(2)}) async-start(f32[8,1,4608]{2,1,0:T(1,128)} %all_to_all.13), calls=%async_computation.1 | async-start | bytes 294912 | tf_op jit(solution)/shard_map/all_to_all | solution.py:558
  115.8 1.1 copy-start.1

commit v3 on v2

--- a/solution.py
+++ b/solution.py
@@ -167,7 +167,7 @@
 
 def composite_kernel(
     slots_ref, first_ref, tab_ref, ord_ref, tgt_ref, wmat_ref, bas_ref, img_ref, gt_ref,
-    p_s, f_s, x_s, m_s, w_s, y_s,
+    p_s, f_s, x_s, m_s, a_s, w_s, h_s, y_s,
 ):
     group = pl.program_id(0)
     length = ord_ref.shape[1]
@@ -235,40 +235,51 @@
             x_s[part, :].astype(jnp.bfloat16), wmat_ref[...], preferred_element_type=jnp.float32
         )
 
+    unroll = 16
+    chunk = unroll * GROUP
+
     def twice(x):
         return jnp.concatenate([x] * (pixels // 128), axis=1)
 
-    def load_colors(r):
-        return [twice(m_s[r, pixels + 128 * ch : pixels + 128 * (ch + 1)]) for ch in range(3)]
-
-    def forward(k, carry):
+    def load_colors(view, r):
+        return [twice(view[r, pixels + 128 * ch : pixels + 128 * (ch + 1)]) for ch in range(3)]
+
+    def views_at(c):
+        part = pl.ds(pl.multiple_of(c * chunk, chunk), chunk)
+        return [ref.at[part, :] for ref in (m_s, a_s, w_s, h_s)]
+
+    def forward(c, carry):
         trans, acc = carry
-        r = pl.ds(pl.multiple_of(k * GROUP, GROUP), GROUP)
-        alpha = jnp.exp(m_s[r, 0:pixels])
-        weight = alpha * trans
-        m_s[r, 0:pixels] = alpha
-        w_s[r, :] = weight
-        colors = load_colors(r)
-        acc = tuple(a + c * weight for a, c in zip(acc, colors))
-        return (trans - weight, acc)
+        m_v, a_v, w_v, _ = views_at(c)
+        for j in range(unroll):
+            r = slice(j * GROUP, (j + 1) * GROUP)
+            alpha = jnp.exp(m_v[r, 0:pixels])
+            weight = alpha * trans
+            a_v[r, :] = alpha
+            w_v[r, :] = weight
+            acc = tuple(a + col * weight for a, col in zip(acc, load_colors(m_v, r)))
+            trans = trans - weight
+        return (trans, acc)
 
     zero = jnp.zeros((GROUP, pixels), jnp.float32)
-    _, image = lax.fori_loop(0, length, forward, (zero + 1.0, (zero, zero, zero)), unroll=16)
+    trips = length // unroll
+    _, image = lax.fori_loop(0, trips, forward, (zero + 1.0, (zero, zero, zero)))
     glist = []
     for ch in range(3):
         img_ref[ch] = image[ch]
         glist.append((image[ch] - tgt_ref[ch]) * (1.0 / pixels))
 
     def backward(i, behind):
-        k = length - 1 - i
-        r = pl.ds(pl.multiple_of(k * GROUP, GROUP), GROUP)
-        c = load_colors(r)
-        delta = (c[0] * glist[0] + c[1] * glist[1] + c[2] * glist[2]) - behind
-        alpha = m_s[r, 0:pixels]
-        m_s[r, 0:pixels] = w_s[r, :] * delta
-        return behind + alpha * delta
-
-    lax.fori_loop(0, length, backward, zero, unroll=16)
+        m_v, a_v, w_v, h_v = views_at(trips - 1 - i)
+        for j in reversed(range(unroll)):
+            r = slice(j * GROUP, (j + 1) * GROUP)
+            c = load_colors(m_v, r)
+            delta = (c[0] * glist[0] + c[1] * glist[1] + c[2] * glist[2]) - behind
+            h_v[r, :] = w_v[r, :] * delta
+            behind = behind + a_v[r, :] * delta
+        return behind
+
+    lax.fori_loop(0, trips, backward, zero)
 
     grows = jnp.concatenate(
         [jnp.zeros((16, pixels), jnp.float32)]
@@ -286,7 +297,7 @@
     @pl.loop(0, steps)
     def _(c):
         part = pl.ds(pl.multiple_of(c * rows, rows), rows)
-        h = m_s[part, 0:pixels]
+        h = h_s[part, :]
         weight = w_s[part, :]
         h1 = h.astype(jnp.bfloat16)
         h2 = (h - h1.astype(jnp.float32)).astype(jnp.bfloat16)
@@ -378,6 +389,8 @@
                 pltpu.VMEM((length * GROUP, 128), jnp.float32),
                 pltpu.VMEM((length * GROUP, pixels + 3 * 128), jnp.float32),
                 pltpu.VMEM((length * GROUP, pixels), jnp.float32),
+                pltpu.VMEM((length * GROUP, pixels), jnp.float32),
+                pltpu.VMEM((length * GROUP, pixels), jnp.float32),
                 pltpu.VMEM((length * GROUP, 128), jnp.float32),
             ],
         ),
@@ -513,6 +526,54 @@
     )(mine)
 
 
+def swap_kernel(cells, mine_ref, out_ref, local_sem, send_sem, recv_sem):
+    me = lax.axis_index("cell")
+    barrier = pltpu.get_barrier_semaphore()
+    peers = [lax.rem(me + step, cells) for step in range(1, cells)]
+    for peer in peers:
+        pl.semaphore_signal(
+            barrier, inc=1, device_id={"cell": peer}, device_id_type=pl.DeviceIdType.MESH
+        )
+    pl.semaphore_wait(barrier, cells - 1)
+    copies = [
+        pltpu.make_async_remote_copy(
+            src_ref=mine_ref.at[peer],
+            dst_ref=out_ref.at[me],
+            send_sem=send_sem.at[step],
+            recv_sem=recv_sem.at[step],
+            device_id={"cell": peer},
+            device_id_type=pl.DeviceIdType.MESH,
+        )
+        for step, peer in enumerate(peers)
+    ]
+    for copy in copies:
+        copy.start()
+    own = pltpu.make_async_copy(mine_ref.at[me], out_ref.at[me], local_sem)
+    own.start()
+    own.wait()
+    for copy in copies:
+        copy.wait()
+
+
+def swap_cells(mine, collective_id):
+    cells = lax.axis_size("cell")
+    blocks = mine.reshape(cells, -1, 128)
+    out = pl.pallas_call(
+        lambda *refs: swap_kernel(cells, *refs),
+        out_shape=jax.ShapeDtypeStruct(blocks.shape, jnp.float32),
+        in_specs=[pl.BlockSpec(memory_space=pl.ANY)],
+        out_specs=pl.BlockSpec(memory_space=pl.ANY),
+        scratch_shapes=[
+            pltpu.SemaphoreType.DMA,
+            pltpu.SemaphoreType.DMA((cells - 1,)),
+            pltpu.SemaphoreType.DMA((cells - 1,)),
+        ],
+        compiler_params=pltpu.CompilerParams(collective_id=collective_id, has_side_effects=True),
+        name=f"swap_cells_{collective_id}",
+    )(blocks)
+    return out.reshape(mine.shape)
+
+
 def local(params, camera, targets, send_blocks, tile_blocks, tile_order):
     cells = lax.axis_size("cell")
     cell_index = lax.axis_index("cell")
@@ -537,7 +598,7 @@
         fields.reshape(FIELDS, owned_blocks, BLOCK_GAUSSIANS), (1, 0, 2)
     ).reshape(owned_blocks, block_values)
     chosen = jnp.take(by_block, picks, axis=0).reshape(cells, per_peer * block_values)
-    received = lax.all_to_all(chosen, "cell", split_axis=0, concat_axis=0, tiled=True)
+    received = swap_cells(chosen, 1)
     received = received.reshape(slots_n, FIELDS, BLOCK_GAUSSIANS)
     dummy = np.zeros((1, FIELDS, BLOCK_GAUSSIANS), np.float32)
     dummy[:, 5] = -1e30
@@ -555,7 +616,7 @@
         .sum(2)
         .reshape(cells, per_peer * block_values)
     )
-    returned = lax.all_to_all(slot_grad, "cell", split_axis=0, concat_axis=0, tiled=True)
+    returned = swap_cells(slot_grad, 2)
     chosen_of = (jnp.arange(owned_blocks)[:, None] == picks[None, :]).astype(jnp.float32)
     summed = jnp.dot(
         chosen_of, returned.reshape(slots_n, block_values), precision=HIGHEST_PRECISE

time: 156 us -> 129 us (0.83)
  Pallas kernels: 113 us -> 103 us
  starting transfers between devices: 8.63 us -> 0 us
  waiting for transfers between devices: 7.36 us -> 0 us
    pallas_call x1, Pallas kernels: 78.2 us -> 56.3 us  [composite(): pl.pallas_call(composite_kernel, out_shape=(jax.ShapeDtypeStruct((3, tile...]
    pallas_call x0 -> x2, Pallas kernels: none -> 11.8 us  [swap_cells(): pl.pallas_call(lambda *refs: swap_kernel(cells, *refs), out_shape=jax.Sha...]
    all_to_all x2 -> x0, starting transfers between devices: 8.63 us -> none  [the longest x1 4.39 us: local(): lax.all_to_all(chosen, 'cell', split_axis=0, concat_axis=0, tiled=True)]
    all_to_all x2 -> x0, waiting for transfers between devices: 7.36 us -> none  [the longest x1 4.67 us: local(): lax.all_to_all(slot_grad, 'cell', split_axis=0, concat_axis=0, tiled=True)]
    another operation x0 -> x4, local copies, waits for them, and re-layouts: none -> 3.35 us  [the longest x2 1.43 us: local(): received = received.reshape(slots_n, FIELDS, BLOCK_GAUSSIANS)]
  transfers between devices with their start and end apart: 2 -> 0, of which waited for: 2 -> 0; matrix products, arithmetic and copies ran while one was open for 1% -> 0% of each run, Pallas kernels for 0% -> 0%
where the time goes in v3:
time: 129 us; the launch traced here: 127 us
  Pallas kernels  103 us (80%)
  local copies, waits for them, and re-layouts  21.4 us (17%)
  other arithmetic  1.54 us (1%)
    pallas_call x1, Pallas kernels, composite(): pl.pallas_call(composite_kernel, out_shape=(jax.ShapeDtypeStruct((3, tile...  56.3 us
    pallas_call x1, Pallas kernels, exchange_views(): pl.pallas_call(lambda *refs: exchange_kernel(views, *refs), out_shape=jax...  23.6 us
    pallas_call x2, Pallas kernels, swap_cells(): pl.pallas_call(lambda *refs: swap_kernel(cells, *refs), out_shape=jax.Sha...  11.8 us
    pallas_call x1, Pallas kernels, local(): pl.pallas_call(pullback_kernel, out_shape=jax.ShapeDtypeStruct((values_n,...  8.07 us
    unnamed x16, local copies, waits for them, and re-layouts  6.33 us
    pallas_call x1, Pallas kernels, local(): pl.pallas_call(project_kernel, out_shape=jax.ShapeDtypeStruct((FIELDS, de...  3 us

profile of v3, /device:TPU:9, one launch (start us, length us, event | category | flops | bytes accessed | tf_op | source)
XLA Modules:
  0.0 126.8 jit_solution(17966370730791872617)
XLA Ops:
  0.6 2.0 %copy.43 = f32[8,8,64,128]{3,2,1,0:T(8,128)S(1)} copy(f32[8,8,64,128]{3,1,2,0:T(8,128)} %bitcast.42) | data formatting | bytes 4194304
  2.6 0.0 copy-start.5
  2.6 1.4 %slice.6.params_ref = f32[59,64,128]{2,1,0:T(8,128)} slice(f32[64,64,128]{2,1,0:T(8,128)S(1)} %bitcast.38), slice={[0:59], [0:64], [0:128]} | slice | bytes 3866624 | tf_op jit(solution)/shard_map/reshape | solution.py:587
  4.0 0.0 copy-done.5
  4.0 0.7 broadcast_in_dim.26.cam_ref
  4.7 3.0 %project.1 = f32[9,64,128]{2,1,0:T(8,128)} custom-call(f32[59,64,128]{2,1,0:T(8,128)} %slice.6.params_ref, f32[16,128]{1,0:T(8,128)} %broadcast_in_dim.26.cam_ref), custom_call_target="tpu_custom_call" | custom-call | tf_op jit(solution)/shard_map/project/pallas_call | solution.py:592
  7.7 0.0 copy-start.3
  7.7 1.3 reshape.73
  8.9 0.3 copy.34
  9.3 0.2 copy.35
  9.5 0.0 copy-done.3
  9.5 0.1 reshape_squeeze.9
  9.6 0.8 gather_fusion
  10.3 0.0 copy-start
  10.3 0.1 reshape_squeeze.8
  10.4 0.1 broadcast_select_fusion
  10.5 0.8 select_n.32.refs_0_
  11.4 6.1 %swap_cells_1.1 = f32[8,36,128]{2,1,0:T(8,128)} custom-call(f32[8,36,128]{2,1,0:T(8,128)} %select_n.32.refs_0_), custom_call_target="tpu_custom_call" | custom-call | tf_op jit(solution)/shard_map/swap_cells_1/pallas_call | solution.py:561
  17.5 1.2 reshape_reshape.10
  18.6 0.3 copy.36
  18.9 0.0 copy-done
  18.9 0.2 tile.4
  19.2 0.0 copy-start.2
  19.2 0.0 copy-start.4
  19.2 1.7 %copy.38.tab_ref = f32[129,16,128]{2,1,0:T(8,128)} copy(f32[129,16,128]{0,2,1:T(8,128)S(1)} %bitcast.36) | data formatting | bytes 2113536 | tf_op jit(solution)/shard_map/tile | solution.py:606
  20.9 0.0 copy-done.2
  20.9 1.3 %copy.37 = s32[4,8,512]{1,2,0:T(8,128)} copy(s32[4,8,512]{2,1,0:T(8,128)S(1)} %bitcast.48) | data formatting | bytes 131072 | tf_op jit(solution)/shard_map/reshape;squeeze | solution.py:355
  22.3 0.0 copy-done.4
  22.3 0.1 copy.33
  22.3 0.6 compare_select_fusion.slots_ref
  22.9 56.3 %shard_map.104 = (f32[3,32,256]{2,1,0:T(8,128)}, f32[129,16,128]{2,1,0:T(8,128)}) custom-call(s32[32,16]{1,0:T(8,128)} %compare_select_fusion.slots_ref, s32[1]{0:T(128)} %bitcast.1.first_ref, f32[129,16,128]{2,1,0:T(8,128)} %copy.38.tab_ref, s32[4,512,8]{2,1,0:T(8,128)} %bitcast.40, f32[3,32,256]{2,1,0:T(8,128)} %bitcast.47, ...), custom_call_target="tpu_custom_call" | custom-call | tf_op jit(solution)/shard_map/pallas_call | solution.py:366
  79.3 1.3 %slice.3 = f32[128,9,128]{2,1,0:T(8,128)S(1)} slice(f32[129,16,128]{2,1,0:T(8,128)} %get-tuple-element.5), slice={[0:128], [0:9], [0:128]} | slice | bytes 1179648 | tf_op jit(solution)/shard_map/slice | solution.py:614
  80.6 0.3 copy.39
  80.9 0.5 copy.40
  81.4 0.9 reshape_reshape.11.refs_0_
  82.3 5.7 %swap_cells_2.1 = f32[8,36,128]{2,1,0:T(8,128)} custom-call(f32[8,36,128]{2,1,0:T(8,128)} %reshape_reshape.11.refs_0_), custom_call_target="tpu_custom_call" | custom-call | tf_op jit(solution)/shard_map/swap_cells_2/pallas_call | solution.py:561
  88.0 1.0 reshape_reshape.12
  89.0 0.0 copy-start.1
  89.1 0.1 copy.41
  89.2 0.3 convolution_bitcast_fusion
  89.5 0.4 copy.42
  89.8 0.3 reshape.76
  90.1 0.0 copy-done.1
  90.2 0.7 pad_maximum_fusion.refs_0_
  90.9 23.6 %exchange_views.1.grads_ref = f32[4,592,128]{2,1,0:T(8,128)} custom-call(f32[592,128]{1,0:T(8,128)} %pad_maximum_fusion.refs_0_), custom_call_target="tpu_custom_call" | custom-call | tf_op jit(solution)/shard_map/exchange_views/pallas_call | solution.py:514
  114.5 8.1 %pullback.1 = f32[59,64,128]{2,1,0:T(8,128)} custom-call(f32[59,64,128]{2,1,0:T(8,128)} %slice.6.params_ref, f32[4,592,128]{2,1,0:T(8,128)} %exchange_views.1.grads_ref), custom_call_target="tpu_custom_call" | custom-call | tf_op jit(solution)/shard_map/pullback/pallas_call | solution.py:628
  122.5 1.7 %pad.17 = f32[64,64,128]{2,1,0:T(8,128)S(1)} pad(f32[59,64,128]{2,1,0:T(8,128)} %pullback.1, f32[]{:T(128)} %constant.33.clone.1), padding=0_5x0_0x0_0 | pad | bytes 4030468
  124.3 2.5 %copy.44 = f32[8,8,64,128]{3,1,2,0:T(8,128)} copy(f32[8,8,64,128]{3,2,1,0:T(8,128)S(1)} %bitcast.37) | data formatting | bytes 4194304
  (6 shorter events, 0.1 us)
Async XLA Ops:
  2.6 1.4 %copy-start.5 = (f32[1,11]{1,0:T(1,128)S(1)}, f32[1,11]{1,0:T(1,128)}, u32[]{:S(2)}) copy-start(f32[1,11]{1,0:T(1,128)} %param.10) | copy-start | bytes 136
  7.7 1.8 %copy-start.3 = (s32[1,1,8,16]{3,2,1,0:T(8,128)S(1)}, s32[1,1,8,16]{3,2,1,0:T(8,128)}, u32[]{:S(2)}) copy-start(s32[1,1,8,16]{3,2,1,0:T(8,128)} %param.12) | copy-start | bytes 1540
  10.3 8.6 %copy-start = (f32[1,9,32]{0,2,1:T(8,128)S(1)}, f32[1,9,32]{0,2,1:T(8,128)}, u32[]{:S(2)}) copy-start(f32[1,9,32]{0,2,1:T(8,128)} %constant.35.clone) | copy-start | bytes 3460
  19.2 1.7 %copy-start.2 = (s32[1,32,512]{2,1,0:T(8,128)S(1)}, s32[1,32,512]{2,1,0:T(8,128)}, u32[]{:S(2)}) copy-start(s32[1,32,512]{2,1,0:T(8,128)} %param.14) | copy-start | bytes 196612
  19.2 3.1 %copy-start.4 = (s32[1,32,16]{1,2,0:T(8,128)S(1)}, s32[1,32,16]{1,2,0:T(8,128)}, u32[]{:S(2)}) copy-start(s32[1,32,16]{1,2,0:T(8,128)} %param.13) | copy-start | bytes 6148
  89.0 1.1 copy-start.1
